TPU v7x, 32 devices: a whole 2x2x4 slice. The times are simulated.
32 devices in a mesh: tm: 16 (over z, y, x), space: 2 (over core).
Axes of the slice: x: 2, y: 2, z: 4, core: 2. Of those that a mesh axis runs over, the one named last changes fastest.
Arguments:
- features: bfloat16 [16, 16, 16, 256], P('tm', 'space'), may hold values from -6 to 6
- masks: int32 [16, 16, 16], P('tm', 'space'), may hold values from 0 to 1
- w_pix: bfloat16 [256, 256], replicated, may hold values from -0.375 to 0.375
- mask_embed: bfloat16 [256], replicated, may hold values from -4 to 4
- w_conv: bfloat16 [3, 3, 256, 256], replicated, may hold values from -0.125 to 0.125
- w_out: bfloat16 [256, 64], replicated, may hold values from -0.375 to 0.375
- w_ptr: bfloat16 [256, 256], replicated, may hold values from -0.375 to 0.375
- w_query: bfloat16 [256, 256], replicated, may hold values from -1 to 1
- w_key: bfloat16 [64, 256], replicated, may hold values from -0.75 to 0.75
- w_value: bfloat16 [64, 256], replicated, may hold values from -0.75 to 0.75
- w_proj: bfloat16 [256, 256], replicated, may hold values from -0.375 to 0.375
- mem_tpos: bfloat16 [3, 64], replicated, may hold values from -120 to 120
- ptr_tpos: bfloat16 [16, 256], replicated, may hold values from -4 to 4
- empty_memory: bfloat16 [64], replicated, may hold values from -4 to 4
Outputs:
- attended: bfloat16 [16, 16, 16, 256], P('tm', 'space')
- memory: bfloat16 [16, 16, 1024], P('tm', 'space')
- pointers: bfloat16 [16, 256], P('tm')
All inputs are finite; a program needn't handle non-finite values.
Results may differ from a plain program's by a relative error of at most 0.015.
The roundings to bfloat16 on the way count: a program that leaves them out, or rounds other values in their place, can miss the bound.
Values may be sent and summed in bfloat16 or wider, within the bound.
A program may use at most 128 MiB of HBM per device.

v0:
```python
import jax
import jax.numpy as jnp
from jax import lax
from jax.sharding import PartitionSpec as P

MEMS = 3
POINTERS = 16


def from_behind(block, axis, distance):
    devices = range(lax.axis_size(axis))
    route = [(i - distance, i) for i in devices if i - distance in devices]
    return lax.ppermute(block, axis, route)


def with_halo(block, sides, width):
    for axis, dim in sides:
        count = lax.axis_size(axis)
        forward = [(i, i + 1) for i in range(count - 1)]
        backward = [(target, source) for source, target in forward]
        low = lax.ppermute(
            lax.slice_in_dim(block, block.shape[dim] - width, None, axis=dim), axis, forward
        )
        high = lax.ppermute(lax.slice_in_dim(block, 0, width, axis=dim), axis, backward)
        block = jnp.concatenate([low, block, high], axis=dim)
    return block


def fetch_earlier(carried, hop_count):
    pieces = []
    for step_index in range(hop_count):
        pieces.append(from_behind(carried, "tm", step_index + 1))
    return jnp.concatenate(pieces[::-1], axis=0)


def attend(query, blocks):
    scores = []
    row_top = None
    for key_rows, value_rows, is_valid in blocks:
        block_scores = lax.dot_general(
            query, key_rows, (((1,), (1,)), ((), ())), preferred_element_type=jnp.float32
        )
        block_scores = jnp.where(is_valid, block_scores, -jnp.inf)
        scores.append(block_scores)
        block_top = jnp.max(block_scores, axis=1, keepdims=True)
        row_top = block_top if row_top is None else jnp.maximum(row_top, block_top)
    row_total = jnp.zeros_like(row_top)
    for block_scores in scores:
        row_total = row_total + jnp.sum(jnp.exp(block_scores - row_top), axis=1, keepdims=True)
    mixed_sum = jnp.zeros((query.shape[0], blocks[0][1].shape[1]), jnp.float32)
    for block_scores, block in zip(scores, blocks):
        weights = (jnp.exp(block_scores - row_top) / row_total).astype(jnp.bfloat16)
        mixed_sum = mixed_sum + jnp.dot(weights, block[1], preferred_element_type=jnp.float32)
    return mixed_sum.astype(jnp.bfloat16)


def body(
    features,
    masks,
    w_pix,
    mask_embed,
    w_conv,
    w_out,
    w_ptr,
    w_query,
    w_key,
    w_value,
    w_proj,
    mem_tpos,
    ptr_tpos,
    empty_memory,
):
    frames_dev, rows_dev, columns, model_dim = features.shape
    mem_dim = w_key.shape[0]
    ptr_tok = model_dim // mem_dim
    band_tokens = rows_dev * columns
    flat_rows = features.reshape(frames_dev * band_tokens, model_dim)
    mask_rows = masks.reshape(frames_dev * band_tokens, 1).astype(jnp.float32)
    joined_map = (
        jnp.dot(flat_rows, w_pix, preferred_element_type=jnp.float32)
        + mask_rows * mask_embed.astype(jnp.float32)
    ).astype(jnp.bfloat16)
    joined_map = joined_map.reshape(frames_dev, rows_dev, columns, model_dim)
    padded = with_halo(joined_map, (("space", 1),), 1)
    padded = jnp.pad(padded, ((0, 0), (0, 0), (1, 1), (0, 0)))
    conv_sum = jnp.zeros((frames_dev * band_tokens, model_dim), jnp.float32)
    for row_tap in range(3):
        for col_tap in range(3):
            window_rows = padded[
                :, row_tap : row_tap + rows_dev, col_tap : col_tap + columns, :
            ].reshape(-1, model_dim)
            conv_sum = conv_sum + jnp.dot(
                window_rows, w_conv[row_tap, col_tap], preferred_element_type=jnp.float32
            )
    hidden = jax.nn.gelu(conv_sum, approximate=True).astype(jnp.bfloat16)
    memory = jnp.dot(hidden, w_out, preferred_element_type=jnp.float32).astype(jnp.bfloat16)
    memory = memory.reshape(frames_dev, rows_dev, columns * mem_dim)
    band_mask = masks.reshape(frames_dev, band_tokens).astype(jnp.bfloat16)
    partial_value = jnp.einsum(
        "ft,ftd->fd",
        band_mask,
        features.reshape(frames_dev, band_tokens, model_dim),
        preferred_element_type=jnp.float32,
    )
    pooled = lax.psum(partial_value, "space")
    normed = (pooled * lax.rsqrt(jnp.mean(pooled * pooled, axis=1, keepdims=True) + 1e-06)).astype(
        jnp.bfloat16
    )
    pointers = jnp.dot(normed, w_ptr, preferred_element_type=jnp.float32).astype(jnp.bfloat16)
    all_pointers = lax.all_gather(pointers, "tm", axis=0, tiled=True)
    hop_count = (MEMS + frames_dev - 1) // frames_dev
    carried = lax.all_gather(memory, "space", axis=1, tiled=True)
    history = jnp.concatenate(
        [fetch_earlier(carried, hop_count), carried[: frames_dev - 1]], axis=0
    )
    grid_tokens = columns * columns
    hist_frames = history.shape[0]
    history = history.reshape(hist_frames, grid_tokens, mem_dim)
    hist_values = jnp.dot(
        history.reshape(-1, mem_dim), w_value, preferred_element_type=jnp.float32
    ).astype(jnp.bfloat16)
    hist_values = hist_values.reshape(hist_frames, grid_tokens, model_dim)
    tpos_keys = jnp.dot(mem_tpos, w_key, preferred_element_type=jnp.float32)
    ptr_tpos_keys = jnp.dot(
        ptr_tpos[::-1].reshape(POINTERS * ptr_tok, mem_dim),
        w_key,
        preferred_element_type=jnp.float32,
    )
    null_key = jnp.dot(
        empty_memory.reshape(1, mem_dim), w_key, preferred_element_type=jnp.float32
    ).astype(jnp.bfloat16)
    null_value = jnp.dot(
        empty_memory.reshape(1, mem_dim), w_value, preferred_element_type=jnp.float32
    ).astype(jnp.bfloat16)
    padded_ptr = jnp.concatenate(
        [jnp.zeros((POINTERS, model_dim), jnp.bfloat16), all_pointers], axis=0
    )
    ptr_offsets = jnp.repeat(jnp.arange(POINTERS, dtype=jnp.int32) - POINTERS, ptr_tok)
    features_f = features.reshape(frames_dev, band_tokens, model_dim).astype(jnp.float32)
    first_frame = lax.axis_index("tm") * frames_dev
    frame = first_frame + 0
    rows_f = features_f[0]
    centred = rows_f - jnp.mean(rows_f, axis=1, keepdims=True)
    query_in = (
        centred * lax.rsqrt(jnp.mean(centred * centred, axis=1, keepdims=True) + 1e-05)
    ).astype(jnp.bfloat16)
    query = (
        jnp.dot(query_in, w_query, preferred_element_type=jnp.float32) * model_dim ** (-0.5)
    ).astype(jnp.bfloat16)
    blocks = []
    for distance in range(1, MEMS + 1):
        slot_index = hop_count * frames_dev - distance
        key_rows = (
            jnp.dot(history[slot_index], w_key, preferred_element_type=jnp.float32)
            + tpos_keys[distance - 1]
        ).astype(jnp.bfloat16)
        blocks.append((key_rows, hist_values[slot_index], frame - distance >= 0))
    window = lax.dynamic_slice_in_dim(padded_ptr, frame, POINTERS, 0)
    ptr_tokens = window.reshape(POINTERS * ptr_tok, mem_dim)
    ptr_keys = (
        jnp.dot(ptr_tokens, w_key, preferred_element_type=jnp.float32) + ptr_tpos_keys
    ).astype(jnp.bfloat16)
    ptr_values = jnp.dot(ptr_tokens, w_value, preferred_element_type=jnp.float32).astype(
        jnp.bfloat16
    )
    extra_valid = jnp.concatenate([frame + ptr_offsets >= 0, jnp.ones((1,), bool)], axis=0)
    blocks.append(
        (
            jnp.concatenate([ptr_keys, null_key], axis=0),
            jnp.concatenate([ptr_values, null_value], axis=0),
            extra_valid[None, :],
        )
    )
    mixed_rows = attend(query, blocks)
    outputs = [
        (rows_f + jnp.dot(mixed_rows, w_proj, preferred_element_type=jnp.float32)).astype(
            jnp.bfloat16
        )
    ]
    attended = jnp.stack(outputs, axis=0).reshape(frames_dev, rows_dev, columns, model_dim)
    return (attended, memory, pointers)


def solution(mesh):
    return jax.shard_map(
        body,
        mesh=mesh,
        in_specs=(
            P("tm", "space", None, None),
            P("tm", "space", None),
            P(),
            P(),
            P(),
            P(),
            P(),
            P(),
            P(),
            P(),
            P(),
            P(),
            P(),
            P(),
        ),
        out_specs=(P("tm", "space", None, None), P("tm", "space", None), P("tm", None)),
        check_vma=False,
    )
```

profile of v0, /device:TPU:24, one launch (start us, length us, event | category | flops | bytes accessed | tf_op | source)
XLA Modules:
  0.0 78.9 jit_solution(8171158523613113094)
XLA Ops:
  0.6 0.0 copy-start
  0.7 0.0 copy-start.7
  0.7 0.0 copy-start.4
  0.7 0.7 convert_element_type.111
  1.4 0.8 convert_bitcast_fusion
  2.2 0.1 convert_element_type.110
  2.3 1.0 %fusion.12 = bf16[128,256]{1,0:T(8,128)(2,1)S(1)} fusion(bf16[128,256]{1,0:T(8,128)(2,1)} %bitcast.107, bf16[256,256]{1,0:T(8,128)(2,1)S(1)} %copy-done, f32[256]{0:T(256)S(1)} %convert_element_type.111, f32[128]{0:T(128)S(1)} %convert_element_type.110), kind=kOutput, calls=%fused_computation.29 | convolution fusion | flops 16875520 | bytes 263680 | tf_op jit(solution)/shard_map/dot_general | solution.py:80
  3.3 1.3 %collective-permute-start.1 = (bf16[1,1,16,256]{3,2,1,0:T(8,128)(2,1)S(1)}, bf16[1,1,16,256]{3,2,1,0:T(8,128)(2,1)S(1)}, u32[]{:S(2)}, u32[]{:S(2)}) collective-permute-start(bf16[1,1,16,256]{3,2,1,0:T(8,128)(2,1)S(1)} %get-tuple-element.15), channel_id=1, source_target_pairs={{1,0},{3,2},{5,4},{7,6},{9,8},{11,10},{13,12},{15,14},{17,16},{19,... | collective-permute-start | bytes 24584 | tf_op jit(solution)/shard_map/ppermute | solution.py:24
  4.6 3.0 %collective-permute-start = (bf16[1,1,16,256]{3,2,1,0:T(8,128)(2,1)S(1)}, bf16[1,1,16,256]{3,2,1,0:T(8,128)(2,1)S(1)}, u32[]{:S(2)}, u32[]{:S(2)}) collective-permute-start(bf16[1,1,16,256]{3,2,1,0:T(8,128)(2,1)S(1)} %get-tuple-element.14), channel_id=1, source_target_pairs={{0,1},{2,3},{4,5},{6,7},{8,9},{10,11},{12,13},{14,15},{16,17},{18,... | collective-permute-start | bytes 24584 | tf_op jit(solution)/shard_map/ppermute | solution.py:21
  7.6 0.9 %convert_reduce_fusion = f32[8,16]{1,0:T(8,128)S(1)} fusion(bf16[1,8,16,256]{3,2,1,0:T(8,128)(2,1)} %param.14), kind=kLoop, calls=%fused_computation.42 | loop fusion | flops 65408 | bytes 66048 | tf_op jit(solution)/shard_map/reduce_sum | solution.py:143
  8.6 1.1 %fusion.22 = f32[8,16]{1,0:T(8,128)S(1)} fusion(bf16[1,8,16,256]{3,2,1,0:T(8,128)(2,1)} %param.14, f32[8,16]{1,0:T(8,128)S(1)} %broadcast_multiply_fusion), kind=kLoop, calls=%fused_computation.50 | loop fusion | flops 130944 | bytes 66560 | tf_op jit(solution)/shard_map/reduce_sum | solution.py:145
  9.7 0.1 div.40
  9.8 0.1 rsqrt.16
  9.8 0.9 %fusion.117 = f32[3,256]{1,0:T(4,128)S(1)} fusion(bf16[3,64]{1,0:T(4,128)(2,1)} %param.25, bf16[64,256]{1,0:T(8,128)(2,1)} %param.22), kind=kOutput, calls=%fused_computation.157 | convolution fusion | flops 98304 | bytes 36224 | tf_op jit(solution)/shard_map/dot_general | solution.py:123
  10.8 0.9 %fusion.100 = f32[1,256]{1,0:T(1,128)S(1)} fusion(bf16[64,256]{1,0:T(8,128)(2,1)} %param.22, bf16[64]{0:T(256)(128)(2,1)} %param.27), kind=kOutput, calls=%fused_computation.138 | convolution fusion | flops 32768 | bytes 33920 | tf_op jit(solution)/shard_map/dot_general | solution.py:129
  11.7 1.0 %convolution_bitcast_fusion = f32[1,256]{1,0:T(1,128)S(1)} fusion(bf16[1,8,16,256]{3,2,1,0:T(8,128)(2,1)} %param.14, bf16[8,16,1]{1,0,2:T(8,128)(2,1)S(1)} %get-tuple-element.19), kind=kOutput, calls=%fused_computation.36 | convolution fusion | flops 65536 | bytes 66816 | tf_op jit(solution)/shard_map/ft,ftd->fd/dot_general | solution.py:99
  12.7 2.4 %psum.7 = f32[1,256]{1,0:T(1,128)S(1)} all-reduce(f32[1,256]{1,0:T(1,128)S(1)} %convolution_bitcast_fusion), channel_id=1, replica_groups=mesh['tm'=16,'space'=2] {'space'}, use_global_device_ids=true, to_apply=%region_5.6 | all-reduce | flops 256 | bytes 2048 | tf_op jit(solution)/shard_map/psum | solution.py:105
  15.2 0.6 multiply_reduce_fusion
  16.5 1.0 %fusion.94 = f32[1,256]{1,0:T(1,128)S(1)} fusion(bf16[256,256]{1,0:T(8,128)(2,1)} %param.20, f32[1,256]{1,0:T(1,128)S(1)} %psum.7, f32[]{:T(128)S(6)} %rsqrt.17), kind=kOutput, calls=%fused_computation.131 | convolution fusion | flops 131584 | bytes 133124 | tf_op jit(solution)/shard_map/dot_general | solution.py:109
  17.5 32.6 %all-gather.1 = bf16[16,1,256]{2,1,0:T(2,128)(2,1)S(1)} all-gather(bf16[1,1,256]{2,1,0:T(2,128)(2,1)S(1)} %reshape.203), channel_id=2, replica_groups=mesh['tm'=16,'space'=2] {'tm'}, dimensions={0}, use_global_device_ids=true | all-gather | bytes 8704 | tf_op jit(solution)/shard_map/all_gather | solution.py:110
  50.1 0.1 reshape.200
  50.2 0.9 %fusion.118 = f32[64,256]{1,0:T(8,128)S(1)} fusion(bf16[64,64]{1,0:T(8,128)(2,1)S(1)} %reshape.200, bf16[64,256]{1,0:T(8,128)(2,1)} %param.22), kind=kOutput, calls=%fused_computation.158 | convolution fusion | flops 2097152 | bytes 106496 | tf_op jit(solution)/shard_map/dot_general | solution.py:161
  51.1 0.7 rev.3
  51.8 0.1 reshape.201
  51.9 0.1 broadcast_in_dim.21
  52.0 0.1 ge.24
  52.1 0.9 %convolution_convert_fusion.1 = bf16[64,256]{1,0:T(8,128)(2,1)S(1)} fusion(bf16[64,64]{1,0:T(8,128)(2,1)S(1)} %reshape.200, bf16[64,256]{1,0:T(8,128)(2,1)} %param.23), kind=kOutput, calls=%fused_computation.33 | convolution fusion | flops 2113536 | bytes 73728 | tf_op jit(solution)/shard_map/dot_general | solution.py:163
  53.0 0.9 %fusion.14 = bf16[64,256]{1,0:T(8,128)(2,1)S(1)} fusion(f32[64,256]{1,0:T(8,128)S(1)} %fusion.118, bf16[64,64]{1,0:T(8,128)(2,1)S(1)} %reshape.201, bf16[64,256]{1,0:T(8,128)(2,1)} %param.22), kind=kOutput, calls=%fused_computation.32 | convolution fusion | flops 2129920 | bytes 139264 | tf_op jit(solution)/shard_map/dot_general | solution.py:124
  53.9 0.1 pad_add_fusion
  54.0 0.2 fusion.11
  54.2 0.2 fusion.113
  54.4 0.1 fusion.98
  54.6 0.2 fusion.35
  54.8 0.2 fusion.45
  55.0 0.2 convolution_add_fusion.13
  55.1 0.2 convolution_add_fusion.12
  55.3 0.2 convolution_add_fusion.11
  55.5 0.2 convolution_add_fusion.10
  55.7 0.2 convolution_add_fusion.9
  55.8 0.2 convolution_add_fusion.8
  56.0 0.3 convolution_convert_fusion.2
  56.4 0.1 copy.19
  56.5 0.1 reshape.196
  56.6 0.0 copy-start.6
  56.6 1.8 %all_gather.6 = bf16[1,16,1024]{2,1,0:T(8,128)(2,1)S(1)} all-gather(bf16[1,8,1024]{2,1,0:T(8,128)(2,1)S(1)} %reshape.196), channel_id=1, replica_groups=mesh['tm'=16,'space'=2] {'space'}, dimensions={1}, use_global_device_ids=true | all-gather | bytes 49152 | tf_op jit(solution)/shard_map/all_gather | solution.py:112
  58.4 3.4 %collective-permute-start.2 = (bf16[1,16,1024]{2,1,0:T(8,128)(2,1)S(1)}, bf16[1,16,1024]{2,1,0:T(8,128)(2,1)S(1)}, u32[]{:S(2)}, u32[]{:S(2)}) collective-permute-start(bf16[1,16,1024]{2,1,0:T(8,128)(2,1)S(1)} %all_gather.6), channel_id=1, source_target_pairs={{0,2},{2,4},{4,6},{6,8},{8,10},{10,12},{12,14},{14,16},{16,18},{18... | collective-permute-start | bytes 98312 | tf_op jit(solution)/shard_map/ppermute | solution.py:13
  61.9 6.1 %collective-permute-start.3 = (bf16[1,16,1024]{2,1,0:T(8,128)(2,1)S(1)}, bf16[1,16,1024]{2,1,0:T(8,128)(2,1)S(1)}, u32[]{:S(2)}, u32[]{:S(2)}) collective-permute-start(bf16[1,16,1024]{2,1,0:T(8,128)(2,1)S(1)} %all_gather.6), channel_id=1, source_target_pairs={{0,4},{2,6},{4,8},{6,10},{8,12},{10,14},{12,16},{14,18},{16,20},{1... | collective-permute-start | bytes 98312 | tf_op jit(solution)/shard_map/ppermute | solution.py:13
  68.0 1.9 %collective-permute-start.4 = (bf16[1,16,1024]{2,1,0:T(8,128)(2,1)S(1)}, bf16[1,16,1024]{2,1,0:T(8,128)(2,1)S(1)}, u32[]{:S(2)}, u32[]{:S(2)}) collective-permute-start(bf16[1,16,1024]{2,1,0:T(8,128)(2,1)S(1)} %all_gather.6), channel_id=1, source_target_pairs={{0,6},{2,8},{4,10},{6,12},{8,14},{10,16},{12,18},{14,20},{16,22},{... | collective-permute-start | bytes 98312 | tf_op jit(solution)/shard_map/ppermute | solution.py:13
  69.9 0.6 convert_element_type.121
  70.5 4.2 %collective-permute-done.4 = bf16[1,16,1024]{2,1,0:T(8,128)(2,1)S(1)} collective-permute-done((bf16[1,16,1024]{2,1,0:T(8,128)(2,1)S(1)}, bf16[1,16,1024]{2,1,0:T(8,128)(2,1)S(1)}, u32[]{:S(2)}, u32[]{:S(2)}) %collective-permute-start.4) | collective-permute-done | bytes 32800 | tf_op jit(solution)/shard_map/ppermute | solution.py:13
  74.7 0.2 reshape_reshape.3
  74.9 0.2 convolution_convert_fusion
  75.1 0.1 squeeze.49
  75.2 0.4 fusion.115
  75.6 0.1 squeeze.51
  75.8 0.4 fusion.114
  76.2 0.1 squeeze.50
  76.3 0.4 fusion.116
  76.8 0.2 fusion.63
  77.1 0.2 fusion.33
  77.3 0.2 convolution_add_fusion.6
  77.5 0.2 convolution_add_fusion.5
  77.8 0.2 copy-done.5
  78.0 1.0 %fusion.13 = bf16[128,256]{1,0:T(8,128)(2,1)} fusion(bf16[256,256]{1,0:T(8,128)(2,1)S(1)} %copy-done.5, f32[128,256]{1,0:T(8,128)S(1)} %convolution_add_fusion.5, bf16[128,256]{1,0:T(8,128)(2,1)S(1)} %bitcast.109, bf16[1,256]{1,0:T(2,128)(2,1)S(1)} %convert_element_type.132, bf16[64,256]{1,0:T(8,128)(2,1)S(1)} %convolution_convert_fusion.1, ...), kind=kOutput, calls=%fused_computation.30 | convolution fusion | flops 21292416 | bytes 460800 | tf_op jit(solution)/shard_map/dot_general | solution.py:176
  (39 shorter events, 0.3 us)
Async XLA Ops:
  0.6 1.6 %copy-start = (bf16[256,256]{1,0:T(8,128)(2,1)S(1)}, bf16[256,256]{1,0:T(8,128)(2,1)}, u32[]{:S(2)}) copy-start(bf16[256,256]{1,0:T(8,128)(2,1)} %param.16) | copy-start | bytes 393220
  0.6 53.3 %copy-start.2 = (bf16[1,8,16,256]{3,2,1,0:T(8,128)(2,1)S(1)}, bf16[1,8,16,256]{3,2,1,0:T(8,128)(2,1)}, u32[]{:S(2)}) copy-start(bf16[1,8,16,256]{3,2,1,0:T(8,128)(2,1)} %param.14) | copy-start | bytes 196612
  0.7 53.7 %copy-start.7 = (bf16[64]{0:T(256)(128)(2,1)S(1)}, bf16[64]{0:T(256)(128)(2,1)}, u32[]{:S(2)}) copy-start(bf16[64]{0:T(256)(128)(2,1)} %param.27) | copy-start | bytes 388
  0.7 53.7 %copy-start.4 = (bf16[64,256]{1,0:T(8,128)(2,1)S(1)}, bf16[64,256]{1,0:T(8,128)(2,1)}, u32[]{:S(2)}) copy-start(bf16[64,256]{1,0:T(8,128)(2,1)} %param.23) | copy-start | bytes 98308
  0.7 53.3 %copy-start.8 = (bf16[256,256]{1,0:T(8,128)(2,1)S(1)}, bf16[256,256]{1,0:T(8,128)(2,1)}, u32[]{:S(2)}) copy-start(bf16[256,256]{1,0:T(8,128)(2,1)} %param.21) | copy-start | bytes 393220
  3.3 51.2 %collective-permute-start.1 = (bf16[1,1,16,256]{3,2,1,0:T(8,128)(2,1)S(1)}, bf16[1,1,16,256]{3,2,1,0:T(8,128)(2,1)S(1)}, u32[]{:S(2)}, u32[]{:S(2)}) collective-permute-start(bf16[1,1,16,256]{3,2,1,0:T(8,128)(2,1)S(1)} %get-tuple-element.15), channel_id=1, source_target_pairs={{1,0},{3,2},{5,4},{7,6},{9,8},{11,10},{13,12},{15,14},{17,16},{19,... | collective-permute-start | bytes 24584 | tf_op jit(solution)/shard_map/ppermute | solution.py:24
  4.6 49.9 %collective-permute-start = (bf16[1,1,16,256]{3,2,1,0:T(8,128)(2,1)S(1)}, bf16[1,1,16,256]{3,2,1,0:T(8,128)(2,1)S(1)}, u32[]{:S(2)}, u32[]{:S(2)}) collective-permute-start(bf16[1,1,16,256]{3,2,1,0:T(8,128)(2,1)S(1)} %get-tuple-element.14), channel_id=1, source_target_pairs={{0,1},{2,3},{4,5},{6,7},{8,9},{10,11},{12,13},{14,15},{16,17},{18,... | collective-permute-start | bytes 24584 | tf_op jit(solution)/shard_map/ppermute | solution.py:21
  8.6 46.0 %copy-start.3 = (bf16[3,3,256,256]{3,2,1,0:T(8,128)(2,1)S(1)}, bf16[3,3,256,256]{3,2,1,0:T(8,128)(2,1)}, u32[]{:S(2)}) copy-start(bf16[3,3,256,256]{3,2,1,0:T(8,128)(2,1)} %param.18) | copy-start | bytes 3538948
  55.1 0.9 %copy-start.9 = (bf16[256,64]{0,1:T(8,128)(2,1)S(1)}, bf16[256,64]{0,1:T(8,128)(2,1)}, u32[]{:S(2)}) copy-start(bf16[256,64]{0,1:T(8,128)(2,1)} %param.19) | copy-start | bytes 98308
  55.8 19.4 %copy-start.1 = (bf16[64,256]{1,0:T(8,128)(2,1)S(1)}, bf16[64,256]{1,0:T(8,128)(2,1)}, u32[]{:S(2)}) copy-start(bf16[64,256]{1,0:T(8,128)(2,1)} %param.22) | copy-start | bytes 98308
  56.6 20.2 %copy-start.6 = (bf16[1,8,1024]{2,1,0:T(8,128)(2,1)}, bf16[1,8,1024]{2,1,0:T(8,128)(2,1)S(1)}, u32[]{:S(2)}) copy-start(bf16[1,8,1024]{2,1,0:T(8,128)(2,1)S(1)} %reshape.196) | copy-start | bytes 49156
  58.4 12.0 %collective-permute-start.2 = (bf16[1,16,1024]{2,1,0:T(8,128)(2,1)S(1)}, bf16[1,16,1024]{2,1,0:T(8,128)(2,1)S(1)}, u32[]{:S(2)}, u32[]{:S(2)}) collective-permute-start(bf16[1,16,1024]{2,1,0:T(8,128)(2,1)S(1)} %all_gather.6), channel_id=1, source_target_pairs={{0,2},{2,4},{4,6},{6,8},{8,10},{10,12},{12,14},{14,16},{16,18},{18... | collective-permute-start | bytes 98312 | tf_op jit(solution)/shard_map/ppermute | solution.py:13
  61.9 8.6 %collective-permute-start.3 = (bf16[1,16,1024]{2,1,0:T(8,128)(2,1)S(1)}, bf16[1,16,1024]{2,1,0:T(8,128)(2,1)S(1)}, u32[]{:S(2)}, u32[]{:S(2)}) collective-permute-start(bf16[1,16,1024]{2,1,0:T(8,128)(2,1)S(1)} %all_gather.6), channel_id=1, source_target_pairs={{0,4},{2,6},{4,8},{6,10},{8,12},{10,14},{12,16},{14,18},{16,20},{1... | collective-permute-start | bytes 98312 | tf_op jit(solution)/shard_map/ppermute | solution.py:13
  68.0 6.7 %collective-permute-start.4 = (bf16[1,16,1024]{2,1,0:T(8,128)(2,1)S(1)}, bf16[1,16,1024]{2,1,0:T(8,128)(2,1)S(1)}, u32[]{:S(2)}, u32[]{:S(2)}) collective-permute-start(bf16[1,16,1024]{2,1,0:T(8,128)(2,1)S(1)} %all_gather.6), channel_id=1, source_target_pairs={{0,6},{2,8},{4,10},{6,12},{8,14},{10,16},{12,18},{14,20},{16,22},{... | collective-permute-start | bytes 98312 | tf_op jit(solution)/shard_map/ppermute | solution.py:13
  77.0 0.9 %copy-start.5 = (bf16[256,256]{1,0:T(8,128)(2,1)S(1)}, bf16[256,256]{1,0:T(8,128)(2,1)}, u32[]{:S(2)}) copy-start(bf16[256,256]{1,0:T(8,128)(2,1)} %param.24) | copy-start | bytes 393220
where the time goes:
time: 79.8 us; the launch traced here: 78.9 us
  blocking collectives  36.9 us (46%)
  starting transfers between devices  15.7 us (20%)
  matrix products  12.9 us (16%)
  other arithmetic  4.59 us (6%)
  waiting for transfers between devices  4.19 us (5%)
  local copies, waits for them, and re-layouts  2.96 us (4%)
  between operations  1.72 us (2%)
    all_gather x1, blocking collectives, body(): all_pointers = lax.all_gather(pointers, 'tm', axis=0, tiled=True)  32.6 us
    ppermute x3, starting transfers between devices, from_behind(): return lax.ppermute(block, axis, route)  11.4 us
    ppermute x3, waiting for transfers between devices, from_behind(): return lax.ppermute(block, axis, route)  4.18 us
    ppermute x1, starting transfers between devices, with_halo(): lax.ppermute(lax.slice_in_dim(block, block.shape[dim] - width, None, axis...  3.03 us
    psum x1, blocking collectives, body(): pooled = lax.psum(partial_value, 'space')  2.45 us
    all_gather x1, blocking collectives, body(): carried = lax.all_gather(memory, 'space', axis=1, tiled=True)  1.83 us
  transfers between devices with their start and end apart: 5, of which 1 were waited for; matrix products, arithmetic and copies ran while one was open for 15% of the time, Pallas kernels for 0%

commit v1 on v0

--- a/solution.py
+++ b/solution.py
@@ -107,7 +107,9 @@
         jnp.bfloat16
     )
     pointers = jnp.dot(normed, w_ptr, preferred_element_type=jnp.float32).astype(jnp.bfloat16)
-    all_pointers = lax.all_gather(pointers, "tm", axis=0, tiled=True)
+    all_pointers = jnp.concatenate(
+        lax.all_to_all(jnp.stack([pointers] * lax.axis_size("tm")), "tm", 0, 0), axis=0
+    )
     hop_count = (MEMS + frames_dev - 1) // frames_dev
     carried = lax.all_gather(memory, "space", axis=1, tiled=True)
     history = jnp.concatenate(

time: 79.8 us -> 52.9 us (0.66)
  the two profiles are of different devices: /device:TPU:24 before, /device:TPU:10 now
where the time goes in v1:
time: 52.9 us; the launch traced here: 52.2 us
  starting transfers between devices  21.6 us (41%)
  matrix products  12.3 us (23%)
  other arithmetic  5.23 us (10%)
  blocking collectives  4.28 us (8%)
  waiting for transfers between devices  3.49 us (7%)
  local copies, waits for them, and re-layouts  3.48 us (7%)
  between operations  1.74 us (3%)
    ppermute x3, starting transfers between devices, from_behind(): return lax.ppermute(block, axis, route)  10.1 us
    all_to_all x1, starting transfers between devices, body(): lax.all_to_all(jnp.stack([pointers] * lax.axis_size('tm')), 'tm', 0, 0)  7.2 us
    ppermute x3, waiting for transfers between devices, from_behind(): return lax.ppermute(block, axis, route)  3.49 us
    ppermute x1, starting transfers between devices, with_halo(): lax.ppermute(lax.slice_in_dim(block, block.shape[dim] - width, None, axis...  3.03 us
    psum x1, blocking collectives, body(): pooled = lax.psum(partial_value, 'space')  2.45 us
    all_gather x1, blocking collectives, body(): carried = lax.all_gather(memory, 'space', axis=1, tiled=True)  1.83 us
    dot_general x4, matrix products, attend(): lax.dot_general(query, key_rows, (((1,), (1,)), ((), ())), preferred_elem...  1.45 us
    dot_general x8, matrix products, body(): jnp.dot(window_rows, w_conv[row_tap, col_tap], preferred_element_type=jnp...  1.32 us
  transfers between devices with their start and end apart: 6, of which 1 were waited for; matrix products, arithmetic and copies ran while one was open for 27% of the time, Pallas kernels for 0%

profile of v1, /device:TPU:10, one launch (start us, length us, event | category | flops | bytes accessed | tf_op | source)
XLA Modules:
  0.0 52.2 jit_solution(10470926022673179398)
XLA Ops:
  0.7 0.8 %convert_element_type.111 = f32[256]{0:T(256)S(1)} convert(bf16[256]{0:T(256)(128)(2,1)} %param.17) | non-fusion elementwise | flops 256 | bytes 1536 | tf_op jit(solution)/shard_map/convert_element_type | solution.py:81
  1.4 0.8 %convert_bitcast_fusion = (bf16[8,16,1]{1,0,2:T(8,128)(2,1)S(1)}, f32[1,8,16]{2,1,0:T(8,128)S(1)}) fusion(s32[1,8,16]{2,1,0:T(8,128)} %param.15), kind=kLoop, calls=%fused_computation.128 | loop fusion | flops 256 | bytes 1280 | tf_op jit(solution)/shard_map/reshape.135
  2.2 0.1 convert_element_type.110
  2.3 1.0 %fusion.12 = bf16[128,256]{1,0:T(8,128)(2,1)S(1)} fusion(bf16[128,256]{1,0:T(8,128)(2,1)} %bitcast.107, bf16[256,256]{1,0:T(8,128)(2,1)S(1)} %copy-done, f32[256]{0:T(256)S(1)} %convert_element_type.111, f32[128]{0:T(128)S(1)} %convert_element_type.110), kind=kOutput, calls=%fused_computation.29 | convolution fusion | flops 16875520 | bytes 263680 | tf_op jit(solution)/shard_map/dot_general | solution.py:80
  3.3 1.3 %collective-permute-start.1 = (bf16[1,1,16,256]{3,2,1,0:T(8,128)(2,1)S(1)}, bf16[1,1,16,256]{3,2,1,0:T(8,128)(2,1)S(1)}, u32[]{:S(2)}, u32[]{:S(2)}) collective-permute-start(bf16[1,1,16,256]{3,2,1,0:T(8,128)(2,1)S(1)} %get-tuple-element.15), channel_id=1, source_target_pairs={{1,0},{3,2},{5,4},{7,6},{9,8},{11,10},{13,12},{15,14},{17,16},{19,... | collective-permute-start | bytes 24584 | tf_op jit(solution)/shard_map/ppermute | solution.py:24
  4.6 3.0 %collective-permute-start = (bf16[1,1,16,256]{3,2,1,0:T(8,128)(2,1)S(1)}, bf16[1,1,16,256]{3,2,1,0:T(8,128)(2,1)S(1)}, u32[]{:S(2)}, u32[]{:S(2)}) collective-permute-start(bf16[1,1,16,256]{3,2,1,0:T(8,128)(2,1)S(1)} %get-tuple-element.14), channel_id=1, source_target_pairs={{0,1},{2,3},{4,5},{6,7},{8,9},{10,11},{12,13},{14,15},{16,17},{18,... | collective-permute-start | bytes 24584 | tf_op jit(solution)/shard_map/ppermute | solution.py:21
  7.6 1.0 %convolution_bitcast_fusion = f32[1,256]{1,0:T(1,128)S(1)} fusion(bf16[1,8,16,256]{3,2,1,0:T(8,128)(2,1)} %param.14, bf16[8,16,1]{1,0,2:T(8,128)(2,1)S(1)} %get-tuple-element.19), kind=kOutput, calls=%fused_computation.36 | convolution fusion | flops 65536 | bytes 66816 | tf_op jit(solution)/shard_map/ft,ftd->fd/dot_general | solution.py:99
  8.7 2.4 %psum.7 = f32[1,256]{1,0:T(1,128)S(1)} all-reduce(f32[1,256]{1,0:T(1,128)S(1)} %convolution_bitcast_fusion), channel_id=1, replica_groups=mesh['tm'=16,'space'=2] {'space'}, use_global_device_ids=true, to_apply=%region_5.6 | all-reduce | flops 256 | bytes 2048 | tf_op jit(solution)/shard_map/psum | solution.py:105
  11.1 0.6 %multiply_reduce_fusion = f32[]{:T(128)} fusion(f32[1,256]{1,0:T(1,128)S(1)} %psum.7), kind=kLoop, calls=%fused_computation.135 | loop fusion | flops 511 | bytes 1028 | tf_op jit(solution)/shard_map/reduce_sum | solution.py:106
  12.4 1.0 %fusion.94 = f32[1,256]{1,0:T(1,128)S(1)} fusion(bf16[256,256]{1,0:T(8,128)(2,1)} %param.20, f32[1,256]{1,0:T(1,128)S(1)} %psum.7, f32[]{:T(128)S(6)} %rsqrt.17), kind=kOutput, calls=%fused_computation.131 | convolution fusion | flops 131584 | bytes 133124 | tf_op jit(solution)/shard_map/dot_general | solution.py:109
  13.5 0.5 broadcast.68
  14.0 0.7 %reduce.3 = bf16[16,256]{1,0:T(8,128)(2,1)S(1)} reduce(bf16[16,1,256]{2,1,0:T(2,128)(2,1)S(1)} %stack.2, bf16[]{:T(256)} %broadcast.68), dimensions={1}, to_apply=%stack.2.reduce_sub_computation | reduce | bytes 16386 | tf_op jit(solution)/shard_map/stack | solution.py:111
  14.7 0.6 %reshape.218 = bf16[16,2,128]{2,1,0:T(2,128)(2,1)} reshape(bf16[16,256]{1,0:T(8,128)(2,1)S(1)} %reduce.3) | data formatting | bytes 16384
  15.3 7.2 %all-to-all-start = ((bf16[16,2,128]{2,1,0:T(2,128)(2,1)}), bf16[16,2,128]{2,1,0:T(2,128)(2,1)S(1)}, u32[]{:S(2)}, u32[]{:S(2)}) async-start(bf16[16,2,128]{2,1,0:T(2,128)(2,1)} %reshape.218), calls=%async_computation | async-start | bytes 16384 | tf_op jit(solution)/shard_map/all_to_all | solution.py:111
  22.5 0.9 %convert_reduce_fusion = f32[8,16]{1,0:T(8,128)S(1)} fusion(bf16[1,8,16,256]{3,2,1,0:T(8,128)(2,1)} %param.14), kind=kLoop, calls=%fused_computation.42 | loop fusion | flops 65408 | bytes 66048 | tf_op jit(solution)/shard_map/reduce_sum | solution.py:145
  23.4 1.0 %fusion.22 = f32[8,16]{1,0:T(8,128)S(1)} fusion(bf16[1,8,16,256]{3,2,1,0:T(8,128)(2,1)} %param.14, f32[8,16]{1,0:T(8,128)S(1)} %broadcast_multiply_fusion), kind=kLoop, calls=%fused_computation.50 | loop fusion | flops 130944 | bytes 66560 | tf_op jit(solution)/shard_map/reduce_sum | solution.py:147
  24.5 0.1 div.40
  24.5 0.1 rsqrt.16
  24.6 0.9 %fusion.117 = f32[3,256]{1,0:T(4,128)S(1)} fusion(bf16[3,64]{1,0:T(4,128)(2,1)} %param.25, bf16[64,256]{1,0:T(8,128)(2,1)} %param.22), kind=kOutput, calls=%fused_computation.157 | convolution fusion | flops 98304 | bytes 36224 | tf_op jit(solution)/shard_map/dot_general | solution.py:125
  25.5 0.9 %fusion.100 = f32[1,256]{1,0:T(1,128)S(1)} fusion(bf16[64,256]{1,0:T(8,128)(2,1)} %param.22, bf16[64]{0:T(256)(128)(2,1)} %param.27), kind=kOutput, calls=%fused_computation.138 | convolution fusion | flops 32768 | bytes 33920 | tf_op jit(solution)/shard_map/dot_general | solution.py:131
  26.4 0.1 broadcast_in_dim.21
  26.5 0.1 ge.24
  26.6 0.9 %fusion.98 = f32[1,256]{1,0:T(1,128)S(1)} fusion(bf16[64,256]{1,0:T(8,128)(2,1)} %param.23, bf16[64]{0:T(256)(128)(2,1)} %param.27), kind=kOutput, calls=%fused_computation.136 | convolution fusion | flops 32768 | bytes 33920 | tf_op jit(solution)/shard_map/dot_general | solution.py:134
  27.5 1.2 %fusion.11 = bf16[128,256]{1,0:T(8,128)(2,1)S(1)} fusion(bf16[256,256]{1,0:T(8,128)(2,1)} %param.21, bf16[128,256]{1,0:T(8,128)(2,1)} %bitcast.108, f32[128]{0:T(128)S(1)} %rsqrt.16, f32[128]{0:T(128)S(1)} %div.40), kind=kOutput, calls=%fused_computation.28 | convolution fusion | flops 16973824 | bytes 263168 | tf_op jit(solution)/shard_map/dot_general | solution.py:150
  28.7 0.1 pad_add_fusion
  28.8 0.6 %convert_element_type.134 = bf16[1,256]{1,0:T(2,128)(2,1)} reshape(bf16[256]{0:T(256)(128)(2,1)S(1)} %convert_element_type.120) | data formatting | bytes 1024 | tf_op jit(solution)/shard_map/convert_element_type | solution.py:109
  29.3 0.1 rev.3
  29.4 0.1 reshape.208
  29.7 0.2 fusion.35
  29.8 0.2 fusion.45
  30.0 0.2 convolution_add_fusion.13
  30.2 0.2 convolution_add_fusion.12
  30.4 0.2 convolution_add_fusion.11
  30.6 0.2 convolution_add_fusion.10
  30.7 0.2 convolution_add_fusion.9
  30.9 0.2 convolution_add_fusion.8
  31.1 0.3 convolution_convert_fusion.2
  31.4 0.1 copy.19
  31.5 0.1 reshape.202
  31.7 1.8 %all_gather.3 = bf16[1,16,1024]{2,1,0:T(8,128)(2,1)S(1)} all-gather(bf16[1,8,1024]{2,1,0:T(8,128)(2,1)S(1)} %reshape.202), channel_id=1, replica_groups=mesh['tm'=16,'space'=2] {'space'}, dimensions={1}, use_global_device_ids=true | all-gather | bytes 49152 | tf_op jit(solution)/shard_map/all_gather | solution.py:114
  33.5 3.4 %collective-permute-start.2 = (bf16[1,16,1024]{2,1,0:T(8,128)(2,1)S(1)}, bf16[1,16,1024]{2,1,0:T(8,128)(2,1)S(1)}, u32[]{:S(2)}, u32[]{:S(2)}) collective-permute-start(bf16[1,16,1024]{2,1,0:T(8,128)(2,1)S(1)} %all_gather.3), channel_id=1, source_target_pairs={{0,2},{2,4},{4,6},{6,8},{8,10},{10,12},{12,14},{14,16},{16,18},{18... | collective-permute-start | bytes 98312 | tf_op jit(solution)/shard_map/ppermute | solution.py:13
  36.9 3.4 %collective-permute-start.3 = (bf16[1,16,1024]{2,1,0:T(8,128)(2,1)S(1)}, bf16[1,16,1024]{2,1,0:T(8,128)(2,1)S(1)}, u32[]{:S(2)}, u32[]{:S(2)}) collective-permute-start(bf16[1,16,1024]{2,1,0:T(8,128)(2,1)S(1)} %all_gather.3), channel_id=1, source_target_pairs={{0,4},{2,6},{4,8},{6,10},{8,12},{10,14},{12,16},{14,18},{16,20},{1... | collective-permute-start | bytes 98312 | tf_op jit(solution)/shard_map/ppermute | solution.py:13
  40.3 3.4 %collective-permute-start.4 = (bf16[1,16,1024]{2,1,0:T(8,128)(2,1)S(1)}, bf16[1,16,1024]{2,1,0:T(8,128)(2,1)S(1)}, u32[]{:S(2)}, u32[]{:S(2)}) collective-permute-start(bf16[1,16,1024]{2,1,0:T(8,128)(2,1)S(1)} %all_gather.3), channel_id=1, source_target_pairs={{0,6},{2,8},{4,10},{6,12},{8,14},{10,16},{12,18},{14,20},{16,22},{... | collective-permute-start | bytes 98312 | tf_op jit(solution)/shard_map/ppermute | solution.py:13
  43.7 0.1 reshape.207
  43.8 0.1 fusion.118
  43.9 0.1 fusion.14
  44.0 0.2 fusion.113
  44.2 0.1 convolution_convert_fusion.1
  44.4 3.5 %collective-permute-done.4 = bf16[1,16,1024]{2,1,0:T(8,128)(2,1)S(1)} collective-permute-done((bf16[1,16,1024]{2,1,0:T(8,128)(2,1)S(1)}, bf16[1,16,1024]{2,1,0:T(8,128)(2,1)S(1)}, u32[]{:S(2)}, u32[]{:S(2)}) %collective-permute-start.4) | collective-permute-done | bytes 32800 | tf_op jit(solution)/shard_map/ppermute | solution.py:13
  47.9 0.2 reshape_reshape.3
  48.1 0.2 convolution_convert_fusion
  48.3 0.1 squeeze.49
  48.4 0.4 fusion.115
  48.8 0.1 squeeze.51
  49.0 0.4 fusion.114
  49.4 0.1 squeeze.50
  49.5 0.4 fusion.116
  50.0 0.2 fusion.63
  50.3 0.2 fusion.33
  50.5 0.2 convolution_add_fusion.6
  50.7 0.2 convolution_add_fusion.5
  51.0 0.1 copy-done.2
  51.1 0.1 copy-done.5
  51.2 1.0 %fusion.13 = bf16[128,256]{1,0:T(8,128)(2,1)} fusion(bf16[256,256]{1,0:T(8,128)(2,1)S(1)} %copy-done.5, f32[128,256]{1,0:T(8,128)S(1)} %convolution_add_fusion.5, bf16[128,256]{1,0:T(8,128)(2,1)S(1)} %bitcast.109, bf16[1,256]{1,0:T(2,128)(2,1)S(1)} %convert_element_type.131, bf16[64,256]{1,0:T(8,128)(2,1)S(1)} %convolution_convert_fusion.1, ...), kind=kOutput, calls=%fused_computation.30 | convolution fusion | flops 21292416 | bytes 460800 | tf_op jit(solution)/shard_map/dot_general | solution.py:178
  (42 shorter events, 0.3 us)
Async XLA Ops:
  0.6 1.6 %copy-start = (bf16[256,256]{1,0:T(8,128)(2,1)S(1)}, bf16[256,256]{1,0:T(8,128)(2,1)}, u32[]{:S(2)}) copy-start(bf16[256,256]{1,0:T(8,128)(2,1)} %param.16) | copy-start | bytes 393220
  0.6 28.7 %copy-start.7 = (bf16[16,256]{1,0:T(8,128)(2,1)S(1)}, bf16[16,256]{1,0:T(8,128)(2,1)}, u32[]{:S(2)}) copy-start(bf16[16,256]{1,0:T(8,128)(2,1)} %param.26) | copy-start | bytes 24580
  0.7 29.0 %copy-start.3 = (bf16[3,3,256,256]{3,2,1,0:T(8,128)(2,1)S(1)}, bf16[3,3,256,256]{3,2,1,0:T(8,128)(2,1)}, u32[]{:S(2)}) copy-start(bf16[3,3,256,256]{3,2,1,0:T(8,128)(2,1)} %param.18) | copy-start | bytes 3538948
  3.3 26.2 %collective-permute-start.1 = (bf16[1,1,16,256]{3,2,1,0:T(8,128)(2,1)S(1)}, bf16[1,1,16,256]{3,2,1,0:T(8,128)(2,1)S(1)}, u32[]{:S(2)}, u32[]{:S(2)}) collective-permute-start(bf16[1,1,16,256]{3,2,1,0:T(8,128)(2,1)S(1)} %get-tuple-element.15), channel_id=1, source_target_pairs={{1,0},{3,2},{5,4},{7,6},{9,8},{11,10},{13,12},{15,14},{17,16},{19,... | collective-permute-start | bytes 24584 | tf_op jit(solution)/shard_map/ppermute | solution.py:24
  4.6 25.0 %collective-permute-start = (bf16[1,1,16,256]{3,2,1,0:T(8,128)(2,1)S(1)}, bf16[1,1,16,256]{3,2,1,0:T(8,128)(2,1)S(1)}, u32[]{:S(2)}, u32[]{:S(2)}) collective-permute-start(bf16[1,1,16,256]{3,2,1,0:T(8,128)(2,1)S(1)} %get-tuple-element.14), channel_id=1, source_target_pairs={{0,1},{2,3},{4,5},{6,7},{8,9},{10,11},{12,13},{14,15},{16,17},{18,... | collective-permute-start | bytes 24584 | tf_op jit(solution)/shard_map/ppermute | solution.py:21
  15.3 28.3 %all-to-all-start = ((bf16[16,2,128]{2,1,0:T(2,128)(2,1)}), bf16[16,2,128]{2,1,0:T(2,128)(2,1)S(1)}, u32[]{:S(2)}, u32[]{:S(2)}) async-start(bf16[16,2,128]{2,1,0:T(2,128)(2,1)} %reshape.218), calls=%async_computation | async-start | bytes 16384 | tf_op jit(solution)/shard_map/all_to_all | solution.py:111
  30.2 0.9 %copy-start.8 = (bf16[256,64]{0,1:T(8,128)(2,1)S(1)}, bf16[256,64]{0,1:T(8,128)(2,1)}, u32[]{:S(2)}) copy-start(bf16[256,64]{0,1:T(8,128)(2,1)} %param.19) | copy-start | bytes 98308
  30.5 13.3 %copy-start.1 = (bf16[64,256]{1,0:T(8,128)(2,1)S(1)}, bf16[64,256]{1,0:T(8,128)(2,1)}, u32[]{:S(2)}) copy-start(bf16[64,256]{1,0:T(8,128)(2,1)} %param.22) | copy-start | bytes 98308
  30.7 13.5 %copy-start.4 = (bf16[64,256]{1,0:T(8,128)(2,1)S(1)}, bf16[64,256]{1,0:T(8,128)(2,1)}, u32[]{:S(2)}) copy-start(bf16[64,256]{1,0:T(8,128)(2,1)} %param.23) | copy-start | bytes 98308
  31.7 17.7 %copy-start.6 = (bf16[1,8,1024]{2,1,0:T(8,128)(2,1)}, bf16[1,8,1024]{2,1,0:T(8,128)(2,1)S(1)}, u32[]{:S(2)}) copy-start(bf16[1,8,1024]{2,1,0:T(8,128)(2,1)S(1)} %reshape.202) | copy-start | bytes 49156
  33.5 10.9 %collective-permute-start.2 = (bf16[1,16,1024]{2,1,0:T(8,128)(2,1)S(1)}, bf16[1,16,1024]{2,1,0:T(8,128)(2,1)S(1)}, u32[]{:S(2)}, u32[]{:S(2)}) collective-permute-start(bf16[1,16,1024]{2,1,0:T(8,128)(2,1)S(1)} %all_gather.3), channel_id=1, source_target_pairs={{0,2},{2,4},{4,6},{6,8},{8,10},{10,12},{12,14},{14,16},{16,18},{18... | collective-permute-start | bytes 98312 | tf_op jit(solution)/shard_map/ppermute | solution.py:13
  36.9 7.5 %collective-permute-start.3 = (bf16[1,16,1024]{2,1,0:T(8,128)(2,1)S(1)}, bf16[1,16,1024]{2,1,0:T(8,128)(2,1)S(1)}, u32[]{:S(2)}, u32[]{:S(2)}) collective-permute-start(bf16[1,16,1024]{2,1,0:T(8,128)(2,1)S(1)} %all_gather.3), channel_id=1, source_target_pairs={{0,4},{2,6},{4,8},{6,10},{8,12},{10,14},{12,16},{14,18},{16,20},{1... | collective-permute-start | bytes 98312 | tf_op jit(solution)/shard_map/ppermute | solution.py:13
  40.3 7.6 %collective-permute-start.4 = (bf16[1,16,1024]{2,1,0:T(8,128)(2,1)S(1)}, bf16[1,16,1024]{2,1,0:T(8,128)(2,1)S(1)}, u32[]{:S(2)}, u32[]{:S(2)}) collective-permute-start(bf16[1,16,1024]{2,1,0:T(8,128)(2,1)S(1)} %all_gather.3), channel_id=1, source_target_pairs={{0,6},{2,8},{4,10},{6,12},{8,14},{10,16},{12,18},{14,20},{16,22},{... | collective-permute-start | bytes 98312 | tf_op jit(solution)/shard_map/ppermute | solution.py:13
  50.2 0.8 %copy-start.2 = (bf16[1,8,16,256]{3,2,1,0:T(8,128)(2,1)S(1)}, bf16[1,8,16,256]{3,2,1,0:T(8,128)(2,1)}, u32[]{:S(2)}) copy-start(bf16[1,8,16,256]{3,2,1,0:T(8,128)(2,1)} %param.14) | copy-start | bytes 196612
  50.2 0.9 %copy-start.5 = (bf16[256,256]{1,0:T(8,128)(2,1)S(1)}, bf16[256,256]{1,0:T(8,128)(2,1)}, u32[]{:S(2)}) copy-start(bf16[256,256]{1,0:T(8,128)(2,1)} %param.24) | copy-start | bytes 393220
